TPU v7x, 32 devices: a whole 2x2x4 slice. The times are simulated.
32 devices in a mesh: replica: 16 (over z, x, core), shard: 2 (over y).
Axes of the slice: x: 2, y: 2, z: 4, core: 2. Of those that a mesh axis runs over, the one named last changes fastest.
Arguments:
- latents: bfloat16 [32, 1024, 1152], P('replica', 'shard'), may hold values from -6 to 6
- conditions: bfloat16 [32, 1152], P('replica'), may hold values from -6 to 6
- cotangent: bfloat16 [32, 1024, 1152], P('replica', 'shard'), may hold values from -6 to 6
- counts: int32 [16], P('replica'), may hold values from 1 to 2, as said below
- w_ada: bfloat16 [1152, 6912], P('shard'), may hold values from -0.1875 to 0.1875
- b_ada: bfloat16 [6912], P('shard'), may hold values from -3 to 3
- w_qkv: bfloat16 [1152, 3456], P('shard'), may hold values from -0.1875 to 0.1875
- b_qv: bfloat16 [2304], P('shard'), may hold values from -3 to 3
- w_proj: bfloat16 [1152, 1152], P('shard'), may hold values from -3.5 to 3.5
- b_proj: bfloat16 [1152], P('shard'), may hold values from -3 to 3
- w_fc1: bfloat16 [1152, 4608], P('shard'), may hold values from -0.1875 to 0.1875
- b_fc1: bfloat16 [4608], P('shard'), may hold values from -3 to 3
- w_fc2: bfloat16 [4608, 1152], P('shard'), may hold values from -0.09375 to 0.09375
- b_fc2: bfloat16 [1152], P('shard'), may hold values from -3 to 3
Outputs:
- output: bfloat16 [32, 1024, 1152], P('replica', 'shard')
- grad_latents: float32 [32, 1024, 1152], P('replica', 'shard')
- grad_conditions: float32 [32, 1152], P('replica')
- grad_w_ada: float32 [1152, 6912], P('shard')
- grad_b_ada: float32 [6912], P('shard')
- grad_w_qkv: float32 [1152, 3456], P('shard')
- grad_b_qv: float32 [2304], P('shard')
- grad_w_proj: float32 [1152, 1152], P('shard')
- grad_b_proj: float32 [1152], P('shard')
- grad_w_fc1: float32 [1152, 4608], P('shard')
- grad_b_fc1: float32 [4608], P('shard')
- grad_w_fc2: float32 [4608, 1152], P('shard')
- grad_b_fc2: float32 [1152], P('shard')
Inputs may be any that keep to these rules, and one draw needn't show every extreme that they name: counts[r] live slots on replica r are its slots 0 to counts[r] - 1 of 2; some replica has all 2 live.
All inputs are finite; a program needn't handle non-finite values.
Results may differ from a plain program's by a relative error of at most 0.019.
Values may be sent and summed in bfloat16 or wider, within the bound.
A program may use at most 512 MiB of HBM per device.

v0:
```python
from functools import partial
import math
import jax
import jax.numpy as jnp
from jax import lax
from jax.sharding import PartitionSpec as P

HEADS = 16
HDIM = 72
epsilon = 1e-06


def layer_stats(values):
    centered = values - jnp.mean(values, axis=-1, keepdims=True)
    inverse = lax.rsqrt(jnp.mean(centered * centered, axis=-1, keepdims=True) + epsilon)
    return (centered * inverse, inverse)


def layer_back(normal, inverse, d_normal):
    first_mean = jnp.mean(d_normal, axis=-1, keepdims=True)
    second_mean = jnp.mean(d_normal * normal, axis=-1, keepdims=True)
    return inverse * (d_normal - first_mean - normal * second_mean)


def contract_last(left, right):
    return lax.dot_general(
        left, right, (((1,), (1,)), ((), ())), preferred_element_type=jnp.float32
    )


def forward_product(inputs, whole_pair):
    return (
        jnp.dot(inputs, whole_pair[0], preferred_element_type=jnp.float32),
        whole_pair[1].astype(jnp.float32),
    )


def backward_product(grads, whole_pair):
    return contract_last(grads, whole_pair[0])


def swap_cores(values):
    return lax.ppermute(values, "core", [(0, 1), (1, 0)])


def join_cores(mine, axis):
    theirs = swap_cores(mine)
    first = lax.axis_index("core") == 0
    return jnp.stack([jnp.where(first, mine, theirs), jnp.where(first, theirs, mine)], axis=axis)


def gather_rows(weight):
    rows, columns = weight.shape
    cores = lax.axis_size("core")
    part = rows // cores
    mine = lax.dynamic_slice_in_dim(weight, lax.axis_index("core") * part, part, 0)
    pieces = lax.all_gather(mine, "shard", axis=0, tiled=False)
    whole = join_cores(pieces, 1)
    return whole.reshape(rows * lax.axis_size("shard"), columns)


def weight_grad(inputs, grads, after):
    n_shard, n_core = (lax.axis_size("shard"), lax.axis_size("core"))
    terms = lax.dot_general(
        inputs, grads, (((0,), (0,)), ((), ())), preferred_element_type=jnp.float32
    ).astype(jnp.bfloat16)
    rows, columns = terms.shape
    part = rows // (n_shard * n_core)
    terms = terms.reshape(n_shard, n_core, part, columns)
    core = lax.axis_index("core")
    keep = lax.dynamic_index_in_dim(terms, core, 1, keepdims=False)
    send = lax.dynamic_index_in_dim(terms, 1 - core, 1, keepdims=False)
    terms = (keep.astype(jnp.float32) + swap_cores(send).astype(jnp.float32)).astype(jnp.bfloat16)
    terms = lax.psum_scatter(terms, "shard", scatter_dimension=0, tiled=True)
    terms = terms.reshape(part, columns)
    if after is not None:
        terms, _ = lax.optimization_barrier((terms, after))
    total = lax.psum(terms, "chip")
    return total


def finish_grad(total):
    joined = join_cores(total, 0).astype(jnp.float32)
    return joined.reshape(2 * total.shape[0], total.shape[1])


def shards(
    latents,
    conditions,
    cotangent,
    counts,
    w_ada,
    b_ada,
    w_qkv,
    b_qv,
    w_proj,
    b_proj,
    w_fc1,
    b_fc1,
    w_fc2,
    b_fc2,
):
    slots, block, width = latents.shape
    n_rows = slots * block
    scale = 1.0 / math.sqrt(HDIM)
    live = (jnp.arange(slots, dtype=jnp.int32) < counts[0]).astype(jnp.float32)[:, None, None]
    index = lax.axis_index("shard")
    biases = (b_ada, b_qv, b_proj, b_fc1, b_fc2)
    bias_all = lax.all_gather(jnp.concatenate(biases), "shard", axis=0, tiled=False)
    full_bias = []
    start = 0
    for bias in biases:
        size = bias.shape[0]
        full_bias.append(bias_all[:, start : start + size].reshape(-1))
        start += size
    full_qkv = (gather_rows(w_qkv), full_bias[1])
    full_proj = (gather_rows(w_proj), full_bias[2])
    full_fc1 = (gather_rows(w_fc1), full_bias[3])
    full_fc2 = (gather_rows(w_fc2), full_bias[4])
    cond_float = conditions.astype(jnp.float32)
    cond_act = jax.nn.silu(cond_float).astype(jnp.bfloat16)
    ada_rows = w_ada.shape[0]
    ada_length = b_ada.shape[0]
    own_cond = lax.dynamic_slice_in_dim(cond_act, index * ada_rows, ada_rows, 1)
    ada_part = jnp.dot(own_cond, w_ada, preferred_element_type=jnp.float32)
    modul = lax.psum(ada_part, "shard") + full_bias[0].astype(jnp.float32)
    shift_a, scale_a, gate_a, shift_m, scale_m, gate_m = [
        piece[:, None, :] for piece in jnp.split(modul, 6, axis=1)
    ]
    tokens = latents.astype(jnp.float32)
    norm_a, inv_a = layer_stats(tokens)
    normed = (norm_a * (1.0 + scale_a) + shift_a).astype(jnp.bfloat16).reshape(n_rows, width)
    qkv_prod, qv_bias = forward_product(normed, full_qkv)
    query = (
        (qkv_prod[:, :width] + qv_bias[:width])
        .astype(jnp.bfloat16)
        .reshape(slots, block, HEADS, HDIM)
    )
    keys_own = qkv_prod[:, width : 2 * width].astype(jnp.bfloat16).reshape(slots, block, width)
    values_own = (
        (qkv_prod[:, 2 * width :] + qv_bias[width:])
        .astype(jnp.bfloat16)
        .reshape(slots, block, width)
    )
    keys_all, values_all = (
        lax.all_gather(keys_own, "shard", axis=1, tiled=True),
        lax.all_gather(values_own, "shard", axis=1, tiled=True),
    )
    length = keys_all.shape[1]
    keys_h = keys_all.reshape(slots, length, HEADS, HDIM)
    values_h = values_all.reshape(slots, length, HEADS, HDIM)
    scores = (
        jnp.einsum("sqhd,skhd->shqk", query, keys_h, preferred_element_type=jnp.float32) * scale
    )
    top_score = jnp.max(scores, axis=-1, keepdims=True)
    log_total = top_score + jnp.log(jnp.sum(jnp.exp(scores - top_score), axis=-1, keepdims=True))
    probs_low = jnp.exp(scores - log_total).astype(jnp.bfloat16)
    attended = jnp.einsum(
        "shqk,skhd->sqhd", probs_low, values_h, preferred_element_type=jnp.float32
    )
    attended_wide = attended
    attended = attended.astype(jnp.bfloat16).reshape(n_rows, width)
    proj_prod, proj_bias = forward_product(attended, full_proj)
    branch_a = (proj_prod + proj_bias).reshape(slots, block, width)
    resid = tokens + gate_a * branch_a
    norm_m, inv_m = layer_stats(resid)
    mixed = (norm_m * (1.0 + scale_m) + shift_m).astype(jnp.bfloat16).reshape(n_rows, width)
    fc1_prod, fc1_bias = forward_product(mixed, full_fc1)
    activated, gelu_back = jax.vjp(partial(jax.nn.gelu, approximate=True), fc1_prod + fc1_bias)
    hidden = activated.astype(jnp.bfloat16)
    fc2_prod, fc2_bias = forward_product(hidden, full_fc2)
    branch_m = (fc2_prod + fc2_bias).reshape(slots, block, width)
    final = resid + gate_m * branch_m
    output = (final * live).astype(jnp.bfloat16)
    d_out = cotangent.astype(jnp.float32) * live
    d_gate_m = jnp.sum(d_out * branch_m, axis=1)
    d_branch_m = (gate_m * d_out).astype(jnp.bfloat16).reshape(n_rows, width)
    sum_fc2 = weight_grad(hidden, d_branch_m, None)
    bias_fc2 = jnp.sum(d_branch_m, axis=0, dtype=jnp.float32)
    d_hidden = backward_product(d_branch_m, full_fc2)
    d_pre = gelu_back(d_hidden)[0].astype(jnp.bfloat16)
    sum_fc1 = weight_grad(mixed, d_pre, sum_fc2)
    bias_fc1 = jnp.sum(d_pre, axis=0, dtype=jnp.float32)
    d_mixed = backward_product(d_pre, full_fc1).reshape(slots, block, width)
    d_shift_m = jnp.sum(d_mixed, axis=1)
    d_scale_m = jnp.sum(d_mixed * norm_m, axis=1)
    d_resid = d_out + layer_back(norm_m, inv_m, d_mixed * (1.0 + scale_m))
    d_gate_a = jnp.sum(d_resid * branch_a, axis=1)
    d_branch_a = (gate_a * d_resid).astype(jnp.bfloat16).reshape(n_rows, width)
    sum_proj = weight_grad(attended, d_branch_a, sum_fc1)
    bias_proj = jnp.sum(d_branch_a, axis=0, dtype=jnp.float32)
    d_attended = (
        backward_product(d_branch_a, full_proj)
        .astype(jnp.bfloat16)
        .reshape(slots, block, HEADS, HDIM)
    )
    scores = (
        jnp.einsum("sqhd,skhd->shqk", query, keys_h, preferred_element_type=jnp.float32) * scale
    )
    probs = jnp.exp(scores - log_total)
    d_probs = jnp.einsum(
        "sqhd,skhd->shqk", d_attended, values_h, preferred_element_type=jnp.float32
    )
    inner = jnp.sum(d_attended.astype(jnp.float32) * attended_wide, axis=-1)
    inner = jnp.swapaxes(inner, 1, 2)[..., None]
    d_scores = (probs * (d_probs - inner)).astype(jnp.bfloat16)
    d_query = (
        (
            jnp.einsum("shqk,skhd->sqhd", d_scores, keys_h, preferred_element_type=jnp.float32)
            * scale
        )
        .astype(jnp.bfloat16)
        .reshape(n_rows, width)
    )
    key_terms = (
        jnp.einsum("shqk,sqhd->skhd", d_scores, query, preferred_element_type=jnp.float32).reshape(
            slots, length, width
        )
        * scale
    )
    value_terms = jnp.einsum(
        "shqk,sqhd->skhd",
        probs.astype(jnp.bfloat16),
        d_attended,
        preferred_element_type=jnp.float32,
    ).reshape(slots, length, width)
    d_keys, d_values = (
        lax.psum_scatter(
            key_terms.astype(jnp.bfloat16), "shard", scatter_dimension=1, tiled=True
        ).astype(jnp.float32),
        lax.psum_scatter(
            value_terms.astype(jnp.bfloat16), "shard", scatter_dimension=1, tiled=True
        ).astype(jnp.float32),
    )
    d_keys = d_keys.astype(jnp.bfloat16).reshape(n_rows, width)
    d_values = d_values.astype(jnp.bfloat16).reshape(n_rows, width)
    d_qkv = jnp.concatenate([d_query, d_keys, d_values], axis=1)
    qv_terms = jnp.concatenate(
        [jnp.sum(d_query, axis=0, dtype=jnp.float32), jnp.sum(d_values, axis=0, dtype=jnp.float32)]
    )
    sum_qkv = weight_grad(normed, d_qkv, sum_proj)
    d_normed = backward_product(d_qkv, full_qkv).reshape(slots, block, width)
    d_shift_a = jnp.sum(d_normed, axis=1)
    d_scale_a = jnp.sum(d_normed * norm_a, axis=1)
    grad_latents = d_resid + layer_back(norm_a, inv_a, d_normed * (1.0 + scale_a))
    d_modul_part = jnp.concatenate(
        [d_shift_a, d_scale_a, d_gate_a, d_shift_m, d_scale_m, d_gate_m], axis=1
    )
    d_modul = lax.psum(d_modul_part, "shard").astype(jnp.bfloat16)
    cond_all = lax.all_gather(own_cond, ("chip", "core"), axis=0, tiled=True)
    d_modul_all = lax.all_gather(d_modul, ("chip", "core"), axis=0, tiled=True)
    grad_w_ada = lax.dot_general(
        cond_all, d_modul_all, (((0,), (0,)), ((), ())), preferred_element_type=jnp.float32
    )
    grad_b_ada = lax.dynamic_slice_in_dim(
        jnp.sum(d_modul_all, axis=0, dtype=jnp.float32), index * ada_length, ada_length, 0
    )
    d_cond_act = lax.all_gather(contract_last(d_modul, w_ada), "shard", axis=1, tiled=True)
    _, silu_back = jax.vjp(jax.nn.silu, cond_float)
    grad_conditions = silu_back(d_cond_act)[0]
    bias_terms = lax.psum(
        jnp.concatenate([qv_terms, bias_proj, bias_fc1, bias_fc2]), ("chip", "core", "shard")
    )
    bias_grads = []
    start = 0
    for bias in biases[1:]:
        size = bias.shape[0]
        bias_grads.append(lax.dynamic_slice_in_dim(bias_terms, start + index * size, size, 0))
        start += size * lax.axis_size("shard")
    return (
        output,
        grad_latents,
        grad_conditions,
        grad_w_ada,
        grad_b_ada,
        finish_grad(sum_qkv),
        bias_grads[0],
        finish_grad(sum_proj),
        bias_grads[1],
        finish_grad(sum_fc1),
        bias_grads[2],
        finish_grad(sum_fc2),
        bias_grads[3],
    )


def solution(mesh):
    names = mesh.axis_names
    n_replica, n_shard = (mesh.shape["replica"], mesh.shape["shard"])
    devices = mesh.devices.transpose(names.index("replica"), names.index("shard"))
    fine = jax.sharding.Mesh(devices.reshape(n_replica // 2, 2, n_shard), ("chip", "core", "shard"))
    placed = (
        P(("chip", "core"), "shard", None),
        P(("chip", "core"), None),
        P(("chip", "core"), "shard", None),
        P(("chip", "core")),
        P("shard", None),
        P("shard"),
        P("shard", None),
        P("shard"),
        P("shard", None),
        P("shard"),
        P("shard", None),
        P("shard"),
        P("shard", None),
        P("shard"),
    )
    return jax.shard_map(
        shards,
        mesh=fine,
        in_specs=placed,
        out_specs=(
            P(("chip", "core"), "shard", None),
            P(("chip", "core"), "shard", None),
            P(("chip", "core"), None),
            P("shard", None),
            P("shard"),
            P("shard", None),
            P("shard"),
            P("shard", None),
            P("shard"),
            P("shard", None),
            P("shard"),
            P("shard", None),
            P("shard"),
        ),
        check_vma=False,
    )
```

profile of v0, /device:TPU:1, one launch (start us, length us, event | category | flops | bytes accessed | tf_op | source)
XLA Modules:
  0.0 1356.5 jit_solution(5749713630772943146)
XLA Ops:
  22.9 44.0 %all-gather.20.cloned.1.call-done = bf16[576,3456]{1,0:T(8,128)(2,1)} async-done(((bf16[288,3456]{1,0:T(8,128)(2,1)}), bf16[576,3456]{1,0:T(8,128)(2,1)}) %all-gather.20.cloned.1.call-update) | async-done | bytes 3981328 | tf_op jit(solution)/shard_map/all_gather | solution.py:57
  89.6 49.3 %all-gather.26.cloned.1.call-done = bf16[2304,1152]{1,0:T(8,128)(2,1)} async-done(((bf16[1152,1152]{1,0:T(8,128)(2,1)}), bf16[2304,1152]{1,0:T(8,128)(2,1)}) %all-gather.26.cloned.1.call-update) | async-done | bytes 5308432 | tf_op jit(solution)/shard_map/all_gather | solution.py:57
  150.9 12.3 fusion.60
  176.3 60.5 %all-gather.24.cloned.1.call-done = bf16[576,4608]{1,0:T(8,128)(2,1)} async-done(((bf16[288,4608]{1,0:T(8,128)(2,1)}), bf16[576,4608]{1,0:T(8,128)(2,1)}) %all-gather.24.cloned.1.call-update) | async-done | bytes 5308432 | tf_op jit(solution)/shard_map/all_gather | solution.py:57
  246.1 9.6 reshape.308
  272.2 9.9 pad_maximum_fusion.1
  291.0 9.3 pad_maximum_fusion
  307.6 27.5 %multiply_reduce_fusion = (f32[2,16,512]{2,1,0:T(8,128)S(1)}, f32[2,16,512,1024]{3,2,1,0:T(8,128)}) fusion(bf16[2,512,16,72]{1,3,2,0:T(8,128)(2,1)} %copy.62, bf16[2,1024,16,72]{1,3,2,0:T(8,128)(2,1)} %bitcast.194), kind=kOutput, calls=%fused_computation.4 | convolution fusion | flops 2449457152 | bytes 74252288 | tf_op jit(solution)/shard_map/sqhd,skhd->shqk/dot_general | solution.py:153
  335.1 21.3 %exponential_reduce_fusion = f32[2,16,512]{2,1,0:T(8,128)S(1)} fusion(f32[2,16,512,1024]{3,2,1,0:T(8,128)} %get-tuple-element.71, f32[2,16,512]{2,1,0:T(8,128)S(1)} %get-tuple-element.70), kind=kLoop, calls=%fused_computation.2 | loop fusion | flops 50315264 | bytes 67239936 | tf_op jit(solution)/shard_map/reduce_sum | solution.py:156
  371.6 28.2 %bitcast_convert_fusion.2 = (bf16[2,512,16,72]{1,3,2,0:T(8,128)(2,1)}, f32[2,16,72,512]{3,2,1,0:T(8,128)}) fusion(bf16[2,1024,16,72]{1,3,2,0:T(8,128)(2,1)} %bitcast.192, f32[2,16,512,1024]{3,2,1,0:T(8,128)} %get-tuple-element.71, f32[2,16,512]{2,1,0:T(8,128)S(1)} %log_add_fusion), kind=kOutput, calls=%fused_computation.77 | convolution fusion | flops 2467430400 | bytes 78970880 | tf_op jit(solution)/shard_map/shqk,skhd->sqhd/dot_general | solution.py:158
  416.2 15.3 %fusion.61 = f32[1024,4608]{1,0:T(8,128)} fusion(bf16[1024,1152]{1,0:T(8,128)(2,1)S(1)} %bitcast.238, bf16[1152,4608]{1,0:T(8,128)(2,1)S(1)} %bitcast.210), kind=kOutput, calls=%fused_computation.179 | convolution fusion | flops 10871635968 | bytes 31850496 | tf_op jit(solution)/shard_map/dot_general | solution.py:33
  431.6 22.7 %convolution_convert_fusion = bf16[4608,1152]{1,0:T(8,128)(2,1)} fusion(bf16[1024,1152]{1,0:T(8,128)(2,1)S(1)} %bitcast.236, f32[1024,4608]{1,0:T(8,128)} %fusion.61, f32[4608]{0:T(1024)S(1)} %reshape.282), kind=kOutput, calls=%fused_computation.7 | convolution fusion | flops 10924130304 | bytes 31868928 | tf_op jit(solution)/shard_map/dot_general | solution.py:64
  460.1 29.3 %convert_reduce_fusion = (f32[4608]{0:T(1024)}, bf16[1024,4608]{1,0:T(8,128)(2,1)}) fusion(f32[1024,4608]{1,0:T(8,128)} %fusion.61, f32[4608]{0:T(1024)S(1)} %reshape.282, bf16[1024,1152]{1,0:T(8,128)(2,1)S(1)} %bitcast.237, bf16[4608,1152]{1,0:T(8,128)(2,1)} %bitcast.205), kind=kOutput, calls=%fused_computation.16 | convolution fusion | flops 10980159488 | bytes 41324544 | tf_op jit(solution)/shard_map/dot_general | solution.py:26
  489.5 21.3 %multiply_reduce_fusion.2 = (f32[2,1152]{1,0:T(2,128)}, f32[2,512]{1,0:T(2,128)S(1)}, f32[2,512]{1,0:T(2,128)S(1)}, f32[2,1152]{1,0:T(2,128)}, f32[2,512,1152]{2,1,0:T(8,128)}) fusion(f32[2,512,1152]{2,1,0:T(8,128)} %copy-done.2, f32[2,512]{1,0:T(2,128)S(1)} %add_rsqrt_fusion, f32[2,512]{1,0:T(2,128)S(1)} %broadcast_multiply_fusion.4, ...), kind=kOutput, calls=%fused_computation.84 | convolution fusion | flops 10882246656 | bytes 29535232 | tf_op jit(solution)/shard_map/dot_general | solution.py:26
  519.2 21.8 %convolution_add_fusion = f32[1024,1152]{1,0:T(8,128)S(1)} fusion(bf16[4608,1152]{1,0:T(8,128)(2,1)} %bitcast.206, f32[1152]{0:T(1024)S(1)} %copy-done.47, f32[1024,4608]{1,0:T(8,128)} %fusion.61, f32[4608]{0:T(1024)S(1)} %reshape.282), kind=kOutput, calls=%fused_computation.62 | convolution fusion | flops 10920001536 | bytes 34232832 | tf_op jit(solution)/shard_map/dot_general | solution.py:33
  556.2 9.6 reshape.309
  577.0 40.1 %multiply_convert_fusion = bf16[2,16,512,1024]{3,2,1,0:T(8,128)(2,1)} fusion(f32[2,16,512,1024]{3,2,1,0:T(8,128)} %get-tuple-element.71, f32[2,16,512]{2,1,0:T(8,128)S(1)} %bitcast.247, f32[2,16,512]{2,1,0:T(8,128)S(1)} %copy-done.12, bf16[2,512,16,72]{1,3,2,0:T(8,128)(2,1)S(1)} %copy-done.5, bf16[2,1024,16,72]{1,3,2,0:T(8,128)(2,1)} %bitcast.193), kind=kOutput, calls=%fused_computation | convolution fusion | flops 2499805184 | bytes 107872256 | tf_op jit(solution)/shard_map/sqhd,skhd->shqk/dot_general | solution.py:201
  617.2 19.4 %multiply_convert_fusion.2 = bf16[2,16,72,1024]{3,2,1,0:T(8,128)(2,1)} fusion(bf16[2,512,16,72]{1,3,2,0:T(8,128)(2,1)} %copy.62, bf16[2,16,512,1024]{3,2,1,0:T(8,128)(2,1)} %multiply_convert_fusion), kind=kOutput, calls=%fused_computation.25 | convolution fusion | flops 2420637696 | bytes 40632320 | tf_op jit(solution)/shard_map/shqk,sqhd->skhd/dot_general | solution.py:216
  643.4 28.0 %fusion.43 = bf16[2,16,72,1024]{3,2,1,0:T(8,128)(2,1)} fusion(bf16[2,512,16,72]{1,3,2,0:T(8,128)(2,1)} %copy.68, f32[2,16,512,1024]{3,2,1,0:T(8,128)} %get-tuple-element.71, f32[2,16,512]{2,1,0:T(8,128)S(1)} %copy-done.12), kind=kOutput, calls=%fused_computation.105 | convolution fusion | flops 2468610048 | bytes 74252288 | tf_op jit(solution)/shard_map/shqk,sqhd->skhd/dot_general | solution.py:221
  678.2 14.8 %convolution_convert_fusion.1 = bf16[1152,4608]{1,0:T(8,128)(2,1)S(1)} fusion(bf16[1024,1152]{1,0:T(8,128)(2,1)} %bitcast.239, bf16[1024,4608]{1,0:T(8,128)(2,1)} %get-tuple-element.32), kind=kOutput, calls=%fused_computation.8 | convolution fusion | flops 10876944384 | bytes 22413312 | tf_op jit(solution)/shard_map/dot_general | solution.py:64
  716.2 18.1 %convert_reduce_fusion.5 = (f32[16,72]{1,0:T(8,128)S(1)}, bf16[2,16,72,512]{3,2,1,0:T(8,128)(2,1)S(1)}) fusion(bf16[2,1024,16,72]{1,3,2,0:T(8,128)(2,1)} %bitcast.195, bf16[2,16,512,1024]{3,2,1,0:T(8,128)(2,1)} %multiply_convert_fusion), kind=kOutput, calls=%fused_computation.82 | convolution fusion | flops 2420636672 | bytes 40636928 | tf_op jit(solution)/shard_map/shqk,skhd->sqhd/dot_general | solution.py:209
  744.7 20.6 %reduce-scatter.9.cloned.1.call-done = bf16[2,512,1152]{2,1,0:T(8,128)(2,1)} async-done(((bf16[2,1024,1152]{2,1,0:T(8,128)(2,1)}), bf16[2,512,1152]{2,1,0:T(8,128)(2,1)}) %reduce-scatter.9.cloned.1.call-update) | async-done | bytes 2359312 | tf_op jit(solution)/shard_map/reduce_scatter | solution.py:231
  769.5 12.2 convolution_convert_fusion.2
  787.9 46.5 %reduce-scatter.15.cloned.1.call-done = bf16[1,288,4608]{2,1,0:T(8,128)(2,1)} async-done(((bf16[2,288,4608]{2,1,0:T(8,128)(2,1)}), bf16[1,288,4608]{2,1,0:T(8,128)(2,1)}) %reduce-scatter.15.cloned.1.call-update) | async-done | bytes 2654224 | tf_op jit(solution)/shard_map/reduce_scatter | solution.py:74
  834.4 118.8 %all-reduce.5.cloned.1.call-done = bf16[1152,1152]{1,0:T(8,128)(2,1)} async-done(((bf16[1152,1152]{1,0:T(8,128)(2,1)}), bf16[1152,1152]{1,0:T(8,128)(2,1)}) %all-reduce.5.cloned.1.call-update) | async-done | bytes 2654224 | tf_op jit(solution)/shard_map/psum | solution.py:78
  953.3 21.4 %all-gather.7 = bf16[16,2,576]{2,1,0:T(2,128)(2,1)S(1)} all-gather(bf16[1,2,576]{2,1,0:T(2,128)(2,1)S(1)} %bitcast.254), channel_id=1, replica_groups=mesh['chip'=8,'core'=2,'shard'=2] {'chip','core'}, dimensions={0}, use_global_device_ids=true | all-gather | bytes 39168 | tf_op jit(solution)/shard_map/all_gather | solution.py:250
  987.6 17.0 %fusion.38 = (f32[2,1152]{1,0:T(2,128)S(1)}, f32[2,512]{1,0:T(2,128)S(1)}, f32[2,512]{1,0:T(2,128)S(1)}, f32[2,1152]{1,0:T(2,128)S(1)}, f32[2,512,1152]{2,1,0:T(8,128)}) fusion(bf16[2,512,1152]{2,1,0:T(8,128)(2,1)} %param.14, f32[2,512]{1,0:T(2,128)S(1)} %copy-done.38, f32[2,512]{1,0:T(2,128)S(1)} %copy-done.32, f32[2,1152]{1,0:T(2,128)S(1)} %copy-done.30, ...), kind=kOutput, calls=%fused_computation.69 | convolution fusion | flops 8186750976 | bytes 22162432 | tf_op jit(solution)/shard_map/dot_general | solution.py:26
  1012.8 37.0 %psum.55 = f32[9216]{0:T(1024)S(1)} all-reduce(f32[9216]{0:T(1024)S(1)} %constant_dynamic-update-slice_fusion.10), channel_id=1, replica_groups=mesh['chip'=8,'core'=2,'shard'=2] {'chip','core','shard'}, use_global_device_ids=true, to_apply=%region_35.36 | all-reduce | flops 9216 | bytes 73728 | tf_op jit(solution)/shard_map/psum | solution.py:261
  1068.3 27.5 %all-gather.8 = bf16[16,2,6912]{2,1,0:T(2,128)(2,1)S(1)} all-gather(bf16[1,2,6912]{2,1,0:T(2,128)(2,1)S(1)} %bitcast.249), channel_id=1, replica_groups=mesh['chip'=8,'core'=2,'shard'=2] {'chip','core'}, dimensions={0}, use_global_device_ids=true | all-gather | bytes 470016 | tf_op jit(solution)/shard_map/all_gather | solution.py:251
  1112.7 43.0 %reduce-scatter.11.cloned.1.call-done = bf16[1,288,3456]{2,1,0:T(8,128)(2,1)} async-done(((bf16[2,288,3456]{2,1,0:T(8,128)(2,1)}), bf16[1,288,3456]{2,1,0:T(8,128)(2,1)}) %reduce-scatter.11.cloned.1.call-update) | async-done | bytes 1990672 | tf_op jit(solution)/shard_map/reduce_scatter | solution.py:74
  1155.7 75.7 %all-reduce.9.cloned.1.call-done = bf16[288,1152]{1,0:T(8,128)(2,1)} async-done(((bf16[288,1152]{1,0:T(8,128)(2,1)}), bf16[288,1152]{1,0:T(8,128)(2,1)}) %all-reduce.9.cloned.1.call-update) | async-done | bytes 663568 | tf_op jit(solution)/shard_map/psum | solution.py:78
  1242.9 91.8 %all-reduce.11.cloned.1.call-done = bf16[288,3456]{1,0:T(8,128)(2,1)} async-done(((bf16[288,3456]{1,0:T(8,128)(2,1)}), bf16[288,3456]{1,0:T(8,128)(2,1)}) %all-reduce.11.cloned.1.call-update) | async-done | bytes 1990672 | tf_op jit(solution)/shard_map/psum | solution.py:78
  (293 shorter events, 316.5 us)
Async XLA Ops:
  7.2 59.7 %all-gather.20.cloned.1.call-start = ((), (), s32[]{:S(2)}) async-start(), calls=%async_computation.18 | async-start | bytes 5971968 | tf_op jit(solution)/shard_map/all_gather | solution.py:57
  10.3 128.6 %all-gather.26.cloned.1.call-start = ((), (), s32[]{:S(2)}) async-start(), calls=%async_computation.21 | async-start | bytes 7962624 | tf_op jit(solution)/shard_map/all_gather | solution.py:57
  14.0 156.5 %all-gather.22.cloned.1.call-start = ((), (), s32[]{:S(2)}) async-start(), calls=%async_computation.19 | async-start | bytes 1990656 | tf_op jit(solution)/shard_map/all_gather | solution.py:57
  14.9 221.9 %all-gather.24.cloned.1.call-start = ((), (), s32[]{:S(2)}) async-start(), calls=%async_computation.20 | async-start | bytes 7962624 | tf_op jit(solution)/shard_map/all_gather | solution.py:57
  18.4 282.5 %all-gather.18.cloned.1.call-start = ((), (), s32[]{:S(2)}) async-start(), calls=%async_computation.7 | async-start | bytes 7077888 | tf_op jit(solution)/shard_map/all_gather | solution.py:146
  66.9 72.7 %collective-permute-start = (bf16[2,288,3456]{2,1,0:T(8,128)(2,1)}, bf16[2,288,3456]{2,1,0:T(8,128)(2,1)}, u32[]{:S(2)}, u32[]{:S(2)}) collective-permute-start(bf16[2,288,3456]{2,1,0:T(8,128)(2,1)} %bitcast.224), channel_id=1, source_target_pairs={{0,2},{2,0},{1,3},{3,1},{4,6},{6,4},{5,7},{7,5},{8,10},{10,8},{9,1... | collective-permute-start | bytes 11943944 | tf_op jit(solution)/shard_map/ppermute | solution.py:43
  84.5 323.9 %copy-start.27 = (f32[2,1152]{1,0:T(2,128)}, f32[2,1152]{1,0:T(2,128)S(1)}, u32[]{:S(2)}) copy-start(f32[2,1152]{1,0:T(2,128)S(1)} %get-tuple-element.65) | copy-start | bytes 27652
  138.9 124.0 %collective-permute-start.3 = (bf16[2,1152,1152]{2,1,0:T(8,128)(2,1)}, bf16[2,1152,1152]{2,1,0:T(8,128)(2,1)}, u32[]{:S(2)}, u32[]{:S(2)}) collective-permute-start(bf16[2,1152,1152]{2,1,0:T(8,128)(2,1)} %bitcast.220), channel_id=1, source_target_pairs={{0,2},{2,0},{1,3},{3,1},{4,6},{6,4},{5,7},{7,5},{8,10},{10,8},{9,1... | collective-permute-start | bytes 15925256 | tf_op jit(solution)/shard_map/ppermute | solution.py:43
  170.3 194.8 %all-gather.16.cloned.1.call-start = ((), (), s32[]{:S(2)}) async-start(), calls=%async_computation.6 | async-start | bytes 7077888 | tf_op jit(solution)/shard_map/all_gather | solution.py:147
  170.5 3.5 collective-permute-start.1
  236.9 45.2 %collective-permute-start.2 = (bf16[2,288,4608]{2,1,0:T(8,128)(2,1)}, bf16[2,288,4608]{2,1,0:T(8,128)(2,1)}, u32[]{:S(2)}, u32[]{:S(2)}) collective-permute-start(bf16[2,288,4608]{2,1,0:T(8,128)(2,1)} %bitcast.222), channel_id=1, source_target_pairs={{0,2},{2,0},{1,3},{3,1},{4,6},{6,4},{5,7},{7,5},{8,10},{10,8},{9,1... | collective-permute-start | bytes 15925256 | tf_op jit(solution)/shard_map/ppermute | solution.py:43
  262.9 453.2 %reduce-scatter.17.cloned.1.call-start = ((), (), s32[]{:S(2)}) async-start(), calls=%async_computation.13 | async-start | bytes 7962624 | tf_op jit(solution)/shard_map/reduce_scatter | solution.py:74
  459.5 51.3 %collective-permute-start.7 = (bf16[2,1152,1152]{2,1,0:T(8,128)(2,1)}, bf16[2,1152,1152]{2,1,0:T(8,128)(2,1)}, u32[]{:S(2)}, u32[]{:S(2)}) collective-permute-start(bf16[2,1152,1152]{2,1,0:T(8,128)(2,1)} %dynamic-slice_bitcast_fusion), channel_id=1, source_target_pairs={{0,2},{2,0},{1,3},{3,1},{4,6},{6,4},{5,7},{7,5},{8,10},{10,8},{9,1... | collective-permute-start | bytes 15925256 | tf_op jit(solution)/shard_map/ppermute | solution.py:43
  518.6 221.8 %reduce-scatter.7.cloned.1.call-start = ((), (), s32[]{:S(2)}) async-start(), calls=%async_computation.8 | async-start | bytes 7077888 | tf_op jit(solution)/shard_map/reduce_scatter | solution.py:228
  643.3 121.9 %reduce-scatter.9.cloned.1.call-start = ((), (), s32[]{:S(2)}) async-start(), calls=%async_computation.9 | async-start | bytes 7077888 | tf_op jit(solution)/shard_map/reduce_scatter | solution.py:231
  678.2 156.2 %reduce-scatter.15.cloned.1.call-start = ((), (), s32[]{:S(2)}) async-start(), calls=%async_computation.12 | async-start | bytes 7962624 | tf_op jit(solution)/shard_map/reduce_scatter | solution.py:74
  693.4 8.9 collective-permute-start.6
  708.6 244.6 %all-reduce.5.cloned.1.call-start = ((), (), s32[]{:S(2)}) async-start(), calls=%async_computation.14 | async-start | bytes 5308416 | tf_op jit(solution)/shard_map/psum | solution.py:78
  715.9 23.0 %collective-permute-start.5 = (bf16[2,288,1152]{2,1,0:T(8,128)(2,1)S(1)}, bf16[2,288,1152]{2,1,0:T(8,128)(2,1)S(1)}, u32[]{:S(2)}, u32[]{:S(2)}) collective-permute-start(bf16[2,288,1152]{2,1,0:T(8,128)(2,1)S(1)} %dynamic-slice_bitcast_fusion.3), channel_id=1, source_target_pairs={{0,2},{2,0},{1,3},{3,1},{4,6},{6,4},{5,7},{7,5},{8,10},{10,8},{9,1... | collective-permute-start | bytes 3981320 | tf_op jit(solution)/shard_map/ppermute | solution.py:43
  716.1 390.1 %reduce-scatter.13.cloned.1.call-start = ((), (), s32[]{:S(2)}) async-start(), calls=%async_computation.11 | async-start | bytes 1990656 | tf_op jit(solution)/shard_map/reduce_scatter | solution.py:74
  740.3 365.9 %all-reduce.7.cloned.1.call-start = ((), (), s32[]{:S(2)}) async-start(), calls=%async_computation.15 | async-start | bytes 5308416 | tf_op jit(solution)/shard_map/psum | solution.py:78
  785.0 168.3 %copy-start.40 = (bf16[2,576]{1,0:T(2,128)(2,1)S(1)}, bf16[2,576]{1,0:T(2,128)(2,1)}, u32[]{:S(2)}) copy-start(bf16[2,576]{1,0:T(2,128)(2,1)} %copy-done.39) | copy-start | bytes 6916
  787.2 191.9 %collective-permute-start.4 = (bf16[2,288,3456]{2,1,0:T(8,128)(2,1)}, bf16[2,288,3456]{2,1,0:T(8,128)(2,1)}, u32[]{:S(2)}, u32[]{:S(2)}) collective-permute-start(bf16[2,288,3456]{2,1,0:T(8,128)(2,1)} %dynamic-slice_bitcast_fusion.2), channel_id=1, source_target_pairs={{0,2},{2,0},{1,3},{3,1},{4,6},{6,4},{5,7},{7,5},{8,10},{10,8},{9,1... | collective-permute-start | bytes 11943944 | tf_op jit(solution)/shard_map/ppermute | solution.py:43
  953.2 202.4 %reduce-scatter.11.cloned.1.call-start = ((), (), s32[]{:S(2)}) async-start(), calls=%async_computation.10 | async-start | bytes 5971968 | tf_op jit(solution)/shard_map/reduce_scatter | solution.py:74
  985.4 246.0 %all-reduce.9.cloned.1.call-start = ((), (), s32[]{:S(2)}) async-start(), calls=%async_computation.16 | async-start | bytes 1327104 | tf_op jit(solution)/shard_map/psum | solution.py:78
  1004.7 46.5 %copy-start.44 = (f32[2,1152]{1,0:T(2,128)S(1)}, f32[2,1152]{1,0:T(2,128)}, u32[]{:S(2)}) copy-start(f32[2,1152]{1,0:T(2,128)} %get-tuple-element.19) | copy-start | bytes 27652
  1004.7 46.5 %copy-start.35 = (f32[2,1152]{1,0:T(2,128)S(1)}, f32[2,1152]{1,0:T(2,128)}, u32[]{:S(2)}) copy-start(f32[2,1152]{1,0:T(2,128)} %get-tuple-element.57) | copy-start | bytes 27652
  1012.6 94.1 %collective-permute-start.11 = (bf16[1152,1152]{1,0:T(8,128)(2,1)}, bf16[1152,1152]{1,0:T(8,128)(2,1)}, u32[]{:S(2)}, u32[]{:S(2)}) collective-permute-start(bf16[1152,1152]{1,0:T(8,128)(2,1)} %all-reduce.5.cloned.1.call-done), channel_id=1, source_target_pairs={{0,2},{2,0},{1,3},{3,1},{4,6},{6,4},{5,7},{7,5},{8,10},{10,8},{9,1... | collective-permute-start | bytes 7962632 | tf_op jit(solution)/shard_map/ppermute | solution.py:43
  1106.3 228.4 %all-reduce.11.cloned.1.call-start = ((), (), s32[]{:S(2)}) async-start(), calls=%async_computation.17 | async-start | bytes 3981312 | tf_op jit(solution)/shard_map/psum | solution.py:78
  1106.5 229.1 %collective-permute-start.10 = (bf16[288,4608]{1,0:T(8,128)(2,1)}, bf16[288,4608]{1,0:T(8,128)(2,1)}, u32[]{:S(2)}, u32[]{:S(2)}) collective-permute-start(bf16[288,4608]{1,0:T(8,128)(2,1)} %all-reduce.7.cloned.1.call-done), channel_id=1, source_target_pairs={{0,2},{2,0},{1,3},{3,1},{4,6},{6,4},{5,7},{7,5},{8,10},{10,8},{9,1... | collective-permute-start | bytes 7962632 | tf_op jit(solution)/shard_map/ppermute | solution.py:43
  1231.4 9.4 collective-permute-start.9
  1334.7 10.2 collective-permute-start.8
  (53 other events, 438.0 us)
Sparse Core Ops, SparseCore 0:
  10.5 56.4 all-gather.19
  69.0 69.8 all-gather.25
  141.1 24.4 all-gather.21
  167.5 69.2 all-gather.23
  238.2 62.6 all-gather.17
  302.3 62.6 all-gather.15
  518.7 65.8 reduce-scatter.16
  643.5 59.3 reduce-scatter.6
  705.2 59.9 reduce-scatter.8
  768.0 66.3 reduce-scatter.14
  838.1 115.0 all-reduce.4
  955.3 23.3 reduce-scatter.12
  982.8 117.3 all-reduce.6
  1103.0 52.5 reduce-scatter.10
  1159.3 72.0 all-reduce.8
  1234.9 99.7 all-reduce.10
where the time goes:
time: 1370 us; the launch traced here: 1360 us
  waiting for transfers between devices  571 us (42%)
  matrix products  360 us (26%)
  other arithmetic  169 us (12%)
  local copies, waits for them, and re-layouts  125 us (9%)
  blocking collectives  108 us (8%)
  between operations  15.9 us (1%)
    psum x4, waiting for transfers between devices, weight_grad(): total = lax.psum(terms, 'chip')  286 us
    all_gather x4, waiting for transfers between devices, gather_rows(): pieces = lax.all_gather(mine, 'shard', axis=0, tiled=False)  154 us
    reduce_scatter x4, waiting for transfers between devices, weight_grad(): terms = lax.psum_scatter(terms, 'shard', scatter_dimension=0, tiled=True)  89.5 us
    dot_general x5, matrix products, contract_last(): lax.dot_general(left, right, (((1,), (1,)), ((), ())), preferred_element_...  77.8 us
    another operation x16, other arithmetic, join_cores(): jnp.stack([jnp.where(first, mine, theirs), jnp.where(first, theirs, mine)...  63.1 us
    dot_general x4, matrix products, weight_grad(): lax.dot_general(inputs, grads, (((0,), (0,)), ((), ())), preferred_elemen...  55.3 us
    dot_general x4, matrix products, forward_product(): jnp.dot(inputs, whole_pair[0], preferred_element_type=jnp.float32)  53.1 us
    dot_general x1, matrix products, shards(): jnp.einsum('sqhd,skhd->shqk', d_attended, values_h, preferred_element_typ...  40.1 us
  transfers between devices with their start and end apart: 28, of which 13 were waited for; matrix products, arithmetic and copies ran while one was open for 39% of the time, Pallas kernels for 0%

commit v1 on v0

--- a/solution.py
+++ b/solution.py
@@ -4,6 +4,7 @@
 import jax.numpy as jnp
 from jax import lax
 from jax.sharding import PartitionSpec as P
+from jax.lax import psum
 
 HEADS = 16
 HDIM = 72
@@ -258,9 +259,8 @@
     d_cond_act = lax.all_gather(contract_last(d_modul, w_ada), "shard", axis=1, tiled=True)
     _, silu_back = jax.vjp(jax.nn.silu, cond_float)
     grad_conditions = silu_back(d_cond_act)[0]
-    bias_terms = lax.psum(
-        jnp.concatenate([qv_terms, bias_proj, bias_fc1, bias_fc2]), ("chip", "core", "shard")
-    )
+    q_in = jnp.concatenate([qv_terms, bias_proj, bias_fc1, bias_fc2])
+    bias_terms = psum(psum(q_in, ("core", "shard")), "chip")
     bias_grads = []
     start = 0
     for bias in biases[1:]:

time: 1370 us -> 1370 us (level)
    psum x1 -> x2, blocking collectives: 37 us -> 39.9 us  [shards(): bias_terms = psum(psum(q_in, ('core', 'shard')), 'chip')]
where the time goes in v1:
time: 1370 us; the launch traced here: 1360 us
  waiting for transfers between devices  565 us (41%)
  matrix products  360 us (26%)
  other arithmetic  169 us (12%)
  local copies, waits for them, and re-layouts  125 us (9%)
  blocking collectives  115 us (8%)
  between operations  15.9 us (1%)
    psum x4, waiting for transfers between devices, weight_grad(): total = lax.psum(terms, 'chip')  286 us
    all_gather x4, waiting for transfers between devices, gather_rows(): pieces = lax.all_gather(mine, 'shard', axis=0, tiled=False)  154 us
    reduce_scatter x4, waiting for transfers between devices, weight_grad(): terms = lax.psum_scatter(terms, 'shard', scatter_dimension=0, tiled=True)  82.8 us
    dot_general x5, matrix products, contract_last(): lax.dot_general(left, right, (((1,), (1,)), ((), ())), preferred_element_...  77.8 us
    another operation x16, other arithmetic, join_cores(): jnp.stack([jnp.where(first, mine, theirs), jnp.where(first, theirs, mine)...  63 us
    dot_general x4, matrix products, weight_grad(): lax.dot_general(inputs, grads, (((0,), (0,)), ((), ())), preferred_elemen...  55.3 us
    dot_general x4, matrix products, forward_product(): jnp.dot(inputs, whole_pair[0], preferred_element_type=jnp.float32)  53.2 us
    dot_general x1, matrix products, shards(): jnp.einsum('sqhd,skhd->shqk', d_attended, values_h, preferred_element_typ...  40.1 us
  transfers between devices with their start and end apart: 28, of which 13 were waited for; matrix products, arithmetic and copies ran while one was open for 39% of the time, Pallas kernels for 0%

profile of v1, /device:TPU:1, one launch (start us, length us, event | category | flops | bytes accessed | tf_op | source)
XLA Modules:
  0.0 1357.0 jit_solution(1884577453902209824)
XLA Ops:
  22.9 44.0 %all-gather.20.cloned.1.call-done = bf16[576,3456]{1,0:T(8,128)(2,1)} async-done(((bf16[288,3456]{1,0:T(8,128)(2,1)}), bf16[576,3456]{1,0:T(8,128)(2,1)}) %all-gather.20.cloned.1.call-update) | async-done | bytes 3981328 | tf_op jit(solution)/shard_map/all_gather | solution.py:58
  89.6 49.3 %all-gather.26.cloned.1.call-done = bf16[2304,1152]{1,0:T(8,128)(2,1)} async-done(((bf16[1152,1152]{1,0:T(8,128)(2,1)}), bf16[2304,1152]{1,0:T(8,128)(2,1)}) %all-gather.26.cloned.1.call-update) | async-done | bytes 5308432 | tf_op jit(solution)/shard_map/all_gather | solution.py:58
  150.9 12.3 fusion.60
  176.3 60.5 %all-gather.24.cloned.1.call-done = bf16[576,4608]{1,0:T(8,128)(2,1)} async-done(((bf16[288,4608]{1,0:T(8,128)(2,1)}), bf16[576,4608]{1,0:T(8,128)(2,1)}) %all-gather.24.cloned.1.call-update) | async-done | bytes 5308432 | tf_op jit(solution)/shard_map/all_gather | solution.py:58
  246.1 9.6 reshape.308
  272.2 9.9 pad_maximum_fusion.1
  307.6 27.5 %multiply_reduce_fusion = (f32[2,16,512]{2,1,0:T(8,128)S(1)}, f32[2,16,512,1024]{3,2,1,0:T(8,128)}) fusion(bf16[2,512,16,72]{1,3,2,0:T(8,128)(2,1)} %copy.62, bf16[2,1024,16,72]{1,3,2,0:T(8,128)(2,1)} %bitcast.194), kind=kOutput, calls=%fused_computation.4 | convolution fusion | flops 2449457152 | bytes 74252288 | tf_op jit(solution)/shard_map/sqhd,skhd->shqk/dot_general | solution.py:154
  335.0 21.3 %exponential_reduce_fusion = f32[2,16,512]{2,1,0:T(8,128)S(1)} fusion(f32[2,16,512,1024]{3,2,1,0:T(8,128)} %get-tuple-element.71, f32[2,16,512]{2,1,0:T(8,128)S(1)} %get-tuple-element.70), kind=kLoop, calls=%fused_computation.2 | loop fusion | flops 50315264 | bytes 67239936 | tf_op jit(solution)/shard_map/reduce_sum | solution.py:157
  371.6 28.2 %bitcast_convert_fusion.2 = (bf16[2,512,16,72]{1,3,2,0:T(8,128)(2,1)}, f32[2,16,72,512]{3,2,1,0:T(8,128)}) fusion(bf16[2,1024,16,72]{1,3,2,0:T(8,128)(2,1)} %bitcast.192, f32[2,16,512,1024]{3,2,1,0:T(8,128)} %get-tuple-element.71, f32[2,16,512]{2,1,0:T(8,128)S(1)} %log_add_fusion), kind=kOutput, calls=%fused_computation.77 | convolution fusion | flops 2467430400 | bytes 78970880 | tf_op jit(solution)/shard_map/shqk,skhd->sqhd/dot_general | solution.py:159
  416.2 15.4 %fusion.61 = f32[1024,4608]{1,0:T(8,128)} fusion(bf16[1024,1152]{1,0:T(8,128)(2,1)S(1)} %bitcast.238, bf16[1152,4608]{1,0:T(8,128)(2,1)S(1)} %bitcast.210), kind=kOutput, calls=%fused_computation.179 | convolution fusion | flops 10871635968 | bytes 31850496 | tf_op jit(solution)/shard_map/dot_general | solution.py:34
  431.6 22.7 %convolution_convert_fusion = bf16[4608,1152]{1,0:T(8,128)(2,1)} fusion(bf16[1024,1152]{1,0:T(8,128)(2,1)S(1)} %bitcast.236, f32[1024,4608]{1,0:T(8,128)} %fusion.61, f32[4608]{0:T(1024)S(1)} %reshape.282), kind=kOutput, calls=%fused_computation.7 | convolution fusion | flops 10924130304 | bytes 31868928 | tf_op jit(solution)/shard_map/dot_general | solution.py:65
  460.2 29.3 %convert_reduce_fusion = (f32[4608]{0:T(1024)}, bf16[1024,4608]{1,0:T(8,128)(2,1)}) fusion(f32[1024,4608]{1,0:T(8,128)} %fusion.61, f32[4608]{0:T(1024)S(1)} %reshape.282, bf16[1024,1152]{1,0:T(8,128)(2,1)S(1)} %bitcast.237, bf16[4608,1152]{1,0:T(8,128)(2,1)} %bitcast.205), kind=kOutput, calls=%fused_computation.16 | convolution fusion | flops 10980159488 | bytes 41324544 | tf_op jit(solution)/shard_map/dot_general | solution.py:27
  489.5 21.3 %multiply_reduce_fusion.2 = (f32[2,1152]{1,0:T(2,128)}, f32[2,512]{1,0:T(2,128)S(1)}, f32[2,512]{1,0:T(2,128)S(1)}, f32[2,1152]{1,0:T(2,128)}, f32[2,512,1152]{2,1,0:T(8,128)}) fusion(f32[2,512,1152]{2,1,0:T(8,128)} %copy-done.2, f32[2,512]{1,0:T(2,128)S(1)} %add_rsqrt_fusion, f32[2,512]{1,0:T(2,128)S(1)} %broadcast_multiply_fusion.4, ...), kind=kOutput, calls=%fused_computation.84 | convolution fusion | flops 10882246656 | bytes 29535232 | tf_op jit(solution)/shard_map/dot_general | solution.py:27
  519.3 21.8 %convolution_add_fusion = f32[1024,1152]{1,0:T(8,128)S(1)} fusion(bf16[4608,1152]{1,0:T(8,128)(2,1)} %bitcast.206, f32[1152]{0:T(1024)S(1)} %copy-done.47, f32[1024,4608]{1,0:T(8,128)} %fusion.61, f32[4608]{0:T(1024)S(1)} %reshape.282), kind=kOutput, calls=%fused_computation.62 | convolution fusion | flops 10920001536 | bytes 34232832 | tf_op jit(solution)/shard_map/dot_general | solution.py:34
  556.2 9.6 reshape.309
  577.0 40.1 %multiply_convert_fusion = bf16[2,16,512,1024]{3,2,1,0:T(8,128)(2,1)} fusion(f32[2,16,512,1024]{3,2,1,0:T(8,128)} %get-tuple-element.71, f32[2,16,512]{2,1,0:T(8,128)S(1)} %bitcast.247, f32[2,16,512]{2,1,0:T(8,128)S(1)} %copy-done.12, bf16[2,512,16,72]{1,3,2,0:T(8,128)(2,1)S(1)} %copy-done.5, bf16[2,1024,16,72]{1,3,2,0:T(8,128)(2,1)} %bitcast.193), kind=kOutput, calls=%fused_computation | convolution fusion | flops 2499805184 | bytes 107872256 | tf_op jit(solution)/shard_map/sqhd,skhd->shqk/dot_general | solution.py:202
  617.1 19.4 %multiply_convert_fusion.2 = bf16[2,16,72,1024]{3,2,1,0:T(8,128)(2,1)} fusion(bf16[2,512,16,72]{1,3,2,0:T(8,128)(2,1)} %copy.62, bf16[2,16,512,1024]{3,2,1,0:T(8,128)(2,1)} %multiply_convert_fusion), kind=kOutput, calls=%fused_computation.25 | convolution fusion | flops 2420637696 | bytes 40632320 | tf_op jit(solution)/shard_map/shqk,sqhd->skhd/dot_general | solution.py:217
  643.4 28.0 %fusion.43 = bf16[2,16,72,1024]{3,2,1,0:T(8,128)(2,1)} fusion(bf16[2,512,16,72]{1,3,2,0:T(8,128)(2,1)} %copy.68, f32[2,16,512,1024]{3,2,1,0:T(8,128)} %get-tuple-element.71, f32[2,16,512]{2,1,0:T(8,128)S(1)} %copy-done.12), kind=kOutput, calls=%fused_computation.105 | convolution fusion | flops 2468610048 | bytes 74252288 | tf_op jit(solution)/shard_map/shqk,sqhd->skhd/dot_general | solution.py:222
  678.2 14.8 %convolution_convert_fusion.1 = bf16[1152,4608]{1,0:T(8,128)(2,1)S(1)} fusion(bf16[1024,1152]{1,0:T(8,128)(2,1)} %bitcast.239, bf16[1024,4608]{1,0:T(8,128)(2,1)} %get-tuple-element.32), kind=kOutput, calls=%fused_computation.8 | convolution fusion | flops 10876944384 | bytes 22413312 | tf_op jit(solution)/shard_map/dot_general | solution.py:65
  716.1 18.1 %convert_reduce_fusion.5 = (f32[16,72]{1,0:T(8,128)S(1)}, bf16[2,16,72,512]{3,2,1,0:T(8,128)(2,1)S(1)}) fusion(bf16[2,1024,16,72]{1,3,2,0:T(8,128)(2,1)} %bitcast.195, bf16[2,16,512,1024]{3,2,1,0:T(8,128)(2,1)} %multiply_convert_fusion), kind=kOutput, calls=%fused_computation.82 | convolution fusion | flops 2420636672 | bytes 40636928 | tf_op jit(solution)/shard_map/shqk,skhd->sqhd/dot_general | solution.py:210
  744.6 20.7 %reduce-scatter.9.cloned.1.call-done = bf16[2,512,1152]{2,1,0:T(8,128)(2,1)} async-done(((bf16[2,1024,1152]{2,1,0:T(8,128)(2,1)}), bf16[2,512,1152]{2,1,0:T(8,128)(2,1)}) %reduce-scatter.9.cloned.1.call-update) | async-done | bytes 2359312 | tf_op jit(solution)/shard_map/reduce_scatter | solution.py:232
  769.6 12.2 convolution_convert_fusion.2
  787.9 46.5 %reduce-scatter.15.cloned.1.call-done = bf16[1,288,4608]{2,1,0:T(8,128)(2,1)} async-done(((bf16[2,288,4608]{2,1,0:T(8,128)(2,1)}), bf16[1,288,4608]{2,1,0:T(8,128)(2,1)}) %reduce-scatter.15.cloned.1.call-update) | async-done | bytes 2654224 | tf_op jit(solution)/shard_map/reduce_scatter | solution.py:75
  834.4 118.8 %all-reduce.5.cloned.1.call-done = bf16[1152,1152]{1,0:T(8,128)(2,1)} async-done(((bf16[1152,1152]{1,0:T(8,128)(2,1)}), bf16[1152,1152]{1,0:T(8,128)(2,1)}) %all-reduce.5.cloned.1.call-update) | async-done | bytes 2654224 | tf_op jit(solution)/shard_map/psum | solution.py:79
  953.3 21.4 %all-gather.7 = bf16[16,2,576]{2,1,0:T(2,128)(2,1)S(1)} all-gather(bf16[1,2,576]{2,1,0:T(2,128)(2,1)S(1)} %bitcast.254), channel_id=1, replica_groups=mesh['chip'=8,'core'=2,'shard'=2] {'chip','core'}, dimensions={0}, use_global_device_ids=true | all-gather | bytes 39168 | tf_op jit(solution)/shard_map/all_gather | solution.py:251
  987.7 17.0 %fusion.38 = (f32[2,1152]{1,0:T(2,128)S(1)}, f32[2,512]{1,0:T(2,128)S(1)}, f32[2,512]{1,0:T(2,128)S(1)}, f32[2,1152]{1,0:T(2,128)S(1)}, f32[2,512,1152]{2,1,0:T(8,128)}) fusion(bf16[2,512,1152]{2,1,0:T(8,128)(2,1)} %param.14, f32[2,512]{1,0:T(2,128)S(1)} %copy-done.38, f32[2,512]{1,0:T(2,128)S(1)} %copy-done.32, f32[2,1152]{1,0:T(2,128)S(1)} %copy-done.30, ...), kind=kOutput, calls=%fused_computation.69 | convolution fusion | flops 8186750976 | bytes 22162432 | tf_op jit(solution)/shard_map/dot_general | solution.py:27
  1012.9 13.1 psum.62
  1025.9 26.8 %psum.63 = f32[9216]{0:T(1024)S(1)} all-reduce(f32[9216]{0:T(1024)S(1)} %psum.62), channel_id=1, replica_groups=mesh['chip'=8,'core'=2,'shard'=2] {'chip'}, use_global_device_ids=true, to_apply=%region_36.37 | all-reduce | flops 9216 | bytes 73728 | tf_op jit(solution)/shard_map/psum | solution.py:263
  1070.1 32.9 %all-gather.8 = bf16[16,2,6912]{2,1,0:T(2,128)(2,1)S(1)} all-gather(bf16[1,2,6912]{2,1,0:T(2,128)(2,1)S(1)} %bitcast.249), channel_id=1, replica_groups=mesh['chip'=8,'core'=2,'shard'=2] {'chip','core'}, dimensions={0}, use_global_device_ids=true | all-gather | bytes 470016 | tf_op jit(solution)/shard_map/all_gather | solution.py:252
  1119.9 36.3 %reduce-scatter.11.cloned.1.call-done = bf16[1,288,3456]{2,1,0:T(8,128)(2,1)} async-done(((bf16[2,288,3456]{2,1,0:T(8,128)(2,1)}), bf16[1,288,3456]{2,1,0:T(8,128)(2,1)}) %reduce-scatter.11.cloned.1.call-update) | async-done | bytes 1990672 | tf_op jit(solution)/shard_map/reduce_scatter | solution.py:75
  1156.2 75.7 %all-reduce.9.cloned.1.call-done = bf16[288,1152]{1,0:T(8,128)(2,1)} async-done(((bf16[288,1152]{1,0:T(8,128)(2,1)}), bf16[288,1152]{1,0:T(8,128)(2,1)}) %all-reduce.9.cloned.1.call-update) | async-done | bytes 663568 | tf_op jit(solution)/shard_map/psum | solution.py:79
  1243.4 91.8 %all-reduce.11.cloned.1.call-done = bf16[288,3456]{1,0:T(8,128)(2,1)} async-done(((bf16[288,3456]{1,0:T(8,128)(2,1)}), bf16[288,3456]{1,0:T(8,128)(2,1)}) %all-reduce.11.cloned.1.call-update) | async-done | bytes 1990672 | tf_op jit(solution)/shard_map/psum | solution.py:79
  (294 shorter events, 324.7 us)
Async XLA Ops:
  7.2 59.7 %all-gather.20.cloned.1.call-start = ((), (), s32[]{:S(2)}) async-start(), calls=%async_computation.18 | async-start | bytes 5971968 | tf_op jit(solution)/shard_map/all_gather | solution.py:58
  10.3 128.6 %all-gather.26.cloned.1.call-start = ((), (), s32[]{:S(2)}) async-start(), calls=%async_computation.21 | async-start | bytes 7962624 | tf_op jit(solution)/shard_map/all_gather | solution.py:58
  14.0 156.6 %all-gather.22.cloned.1.call-start = ((), (), s32[]{:S(2)}) async-start(), calls=%async_computation.19 | async-start | bytes 1990656 | tf_op jit(solution)/shard_map/all_gather | solution.py:58
  14.9 221.9 %all-gather.24.cloned.1.call-start = ((), (), s32[]{:S(2)}) async-start(), calls=%async_computation.20 | async-start | bytes 7962624 | tf_op jit(solution)/shard_map/all_gather | solution.py:58
  18.4 282.5 %all-gather.18.cloned.1.call-start = ((), (), s32[]{:S(2)}) async-start(), calls=%async_computation.7 | async-start | bytes 7077888 | tf_op jit(solution)/shard_map/all_gather | solution.py:147
  66.9 72.7 %collective-permute-start = (bf16[2,288,3456]{2,1,0:T(8,128)(2,1)}, bf16[2,288,3456]{2,1,0:T(8,128)(2,1)}, u32[]{:S(2)}, u32[]{:S(2)}) collective-permute-start(bf16[2,288,3456]{2,1,0:T(8,128)(2,1)} %bitcast.224), channel_id=1, source_target_pairs={{0,2},{2,0},{1,3},{3,1},{4,6},{6,4},{5,7},{7,5},{8,10},{10,8},{9,1... | collective-permute-start | bytes 11943944 | tf_op jit(solution)/shard_map/ppermute | solution.py:44
  84.5 323.9 %copy-start.27 = (f32[2,1152]{1,0:T(2,128)}, f32[2,1152]{1,0:T(2,128)S(1)}, u32[]{:S(2)}) copy-start(f32[2,1152]{1,0:T(2,128)S(1)} %get-tuple-element.65) | copy-start | bytes 27652
  138.9 124.0 %collective-permute-start.3 = (bf16[2,1152,1152]{2,1,0:T(8,128)(2,1)}, bf16[2,1152,1152]{2,1,0:T(8,128)(2,1)}, u32[]{:S(2)}, u32[]{:S(2)}) collective-permute-start(bf16[2,1152,1152]{2,1,0:T(8,128)(2,1)} %bitcast.220), channel_id=1, source_target_pairs={{0,2},{2,0},{1,3},{3,1},{4,6},{6,4},{5,7},{7,5},{8,10},{10,8},{9,1... | collective-permute-start | bytes 15925256 | tf_op jit(solution)/shard_map/ppermute | solution.py:44
  170.3 194.7 %all-gather.16.cloned.1.call-start = ((), (), s32[]{:S(2)}) async-start(), calls=%async_computation.6 | async-start | bytes 7077888 | tf_op jit(solution)/shard_map/all_gather | solution.py:148
  170.5 3.5 collective-permute-start.1
  236.9 45.2 %collective-permute-start.2 = (bf16[2,288,4608]{2,1,0:T(8,128)(2,1)}, bf16[2,288,4608]{2,1,0:T(8,128)(2,1)}, u32[]{:S(2)}, u32[]{:S(2)}) collective-permute-start(bf16[2,288,4608]{2,1,0:T(8,128)(2,1)} %bitcast.222), channel_id=1, source_target_pairs={{0,2},{2,0},{1,3},{3,1},{4,6},{6,4},{5,7},{7,5},{8,10},{10,8},{9,1... | collective-permute-start | bytes 15925256 | tf_op jit(solution)/shard_map/ppermute | solution.py:44
  262.9 453.1 %reduce-scatter.17.cloned.1.call-start = ((), (), s32[]{:S(2)}) async-start(), calls=%async_computation.13 | async-start | bytes 7962624 | tf_op jit(solution)/shard_map/reduce_scatter | solution.py:75
  459.5 51.3 %collective-permute-start.7 = (bf16[2,1152,1152]{2,1,0:T(8,128)(2,1)}, bf16[2,1152,1152]{2,1,0:T(8,128)(2,1)}, u32[]{:S(2)}, u32[]{:S(2)}) collective-permute-start(bf16[2,1152,1152]{2,1,0:T(8,128)(2,1)} %dynamic-slice_bitcast_fusion), channel_id=1, source_target_pairs={{0,2},{2,0},{1,3},{3,1},{4,6},{6,4},{5,7},{7,5},{8,10},{10,8},{9,1... | collective-permute-start | bytes 15925256 | tf_op jit(solution)/shard_map/ppermute | solution.py:44
  518.6 221.6 %reduce-scatter.7.cloned.1.call-start = ((), (), s32[]{:S(2)}) async-start(), calls=%async_computation.8 | async-start | bytes 7077888 | tf_op jit(solution)/shard_map/reduce_scatter | solution.py:229
  643.3 122.0 %reduce-scatter.9.cloned.1.call-start = ((), (), s32[]{:S(2)}) async-start(), calls=%async_computation.9 | async-start | bytes 7077888 | tf_op jit(solution)/shard_map/reduce_scatter | solution.py:232
  678.1 156.3 %reduce-scatter.15.cloned.1.call-start = ((), (), s32[]{:S(2)}) async-start(), calls=%async_computation.12 | async-start | bytes 7962624 | tf_op jit(solution)/shard_map/reduce_scatter | solution.py:75
  693.3 8.9 collective-permute-start.6
  708.5 244.7 %all-reduce.5.cloned.1.call-start = ((), (), s32[]{:S(2)}) async-start(), calls=%async_computation.14 | async-start | bytes 5308416 | tf_op jit(solution)/shard_map/psum | solution.py:79
  715.8 22.9 %collective-permute-start.5 = (bf16[2,288,1152]{2,1,0:T(8,128)(2,1)S(1)}, bf16[2,288,1152]{2,1,0:T(8,128)(2,1)S(1)}, u32[]{:S(2)}, u32[]{:S(2)}) collective-permute-start(bf16[2,288,1152]{2,1,0:T(8,128)(2,1)S(1)} %dynamic-slice_bitcast_fusion.3), channel_id=1, source_target_pairs={{0,2},{2,0},{1,3},{3,1},{4,6},{6,4},{5,7},{7,5},{8,10},{10,8},{9,1... | collective-permute-start | bytes 3981320 | tf_op jit(solution)/shard_map/ppermute | solution.py:44
  716.1 397.4 %reduce-scatter.13.cloned.1.call-start = ((), (), s32[]{:S(2)}) async-start(), calls=%async_computation.11 | async-start | bytes 1990656 | tf_op jit(solution)/shard_map/reduce_scatter | solution.py:75
  740.2 373.3 %all-reduce.7.cloned.1.call-start = ((), (), s32[]{:S(2)}) async-start(), calls=%async_computation.15 | async-start | bytes 5308416 | tf_op jit(solution)/shard_map/psum | solution.py:79
  785.0 168.3 %copy-start.40 = (bf16[2,576]{1,0:T(2,128)(2,1)S(1)}, bf16[2,576]{1,0:T(2,128)(2,1)}, u32[]{:S(2)}) copy-start(bf16[2,576]{1,0:T(2,128)(2,1)} %copy-done.39) | copy-start | bytes 6916
  787.3 194.0 %collective-permute-start.4 = (bf16[2,288,3456]{2,1,0:T(8,128)(2,1)}, bf16[2,288,3456]{2,1,0:T(8,128)(2,1)}, u32[]{:S(2)}, u32[]{:S(2)}) collective-permute-start(bf16[2,288,3456]{2,1,0:T(8,128)(2,1)} %dynamic-slice_bitcast_fusion.2), channel_id=1, source_target_pairs={{0,2},{2,0},{1,3},{3,1},{4,6},{6,4},{5,7},{7,5},{8,10},{10,8},{9,1... | collective-permute-start | bytes 11943944 | tf_op jit(solution)/shard_map/ppermute | solution.py:44
  953.3 202.9 %reduce-scatter.11.cloned.1.call-start = ((), (), s32[]{:S(2)}) async-start(), calls=%async_computation.10 | async-start | bytes 5971968 | tf_op jit(solution)/shard_map/reduce_scatter | solution.py:75
  987.5 244.4 %all-reduce.9.cloned.1.call-start = ((), (), s32[]{:S(2)}) async-start(), calls=%async_computation.16 | async-start | bytes 1327104 | tf_op jit(solution)/shard_map/psum | solution.py:79
  1004.7 49.4 %copy-start.44 = (f32[2,1152]{1,0:T(2,128)S(1)}, f32[2,1152]{1,0:T(2,128)}, u32[]{:S(2)}) copy-start(f32[2,1152]{1,0:T(2,128)} %get-tuple-element.19) | copy-start | bytes 27652
  1004.8 49.4 %copy-start.35 = (f32[2,1152]{1,0:T(2,128)S(1)}, f32[2,1152]{1,0:T(2,128)}, u32[]{:S(2)}) copy-start(f32[2,1152]{1,0:T(2,128)} %get-tuple-element.57) | copy-start | bytes 27652
  1012.8 101.2 %collective-permute-start.11 = (bf16[1152,1152]{1,0:T(8,128)(2,1)}, bf16[1152,1152]{1,0:T(8,128)(2,1)}, u32[]{:S(2)}, u32[]{:S(2)}) collective-permute-start(bf16[1152,1152]{1,0:T(8,128)(2,1)} %all-reduce.5.cloned.1.call-done), channel_id=1, source_target_pairs={{0,2},{2,0},{1,3},{3,1},{4,6},{6,4},{5,7},{7,5},{8,10},{10,8},{9,1... | collective-permute-start | bytes 7962632 | tf_op jit(solution)/shard_map/ppermute | solution.py:44
  1113.5 221.7 %all-reduce.11.cloned.1.call-start = ((), (), s32[]{:S(2)}) async-start(), calls=%async_computation.17 | async-start | bytes 3981312 | tf_op jit(solution)/shard_map/psum | solution.py:79
  1113.7 222.4 %collective-permute-start.10 = (bf16[288,4608]{1,0:T(8,128)(2,1)}, bf16[288,4608]{1,0:T(8,128)(2,1)}, u32[]{:S(2)}, u32[]{:S(2)}) collective-permute-start(bf16[288,4608]{1,0:T(8,128)(2,1)} %all-reduce.7.cloned.1.call-done), channel_id=1, source_target_pairs={{0,2},{2,0},{1,3},{3,1},{4,6},{6,4},{5,7},{7,5},{8,10},{10,8},{9,1... | collective-permute-start | bytes 7962632 | tf_op jit(solution)/shard_map/ppermute | solution.py:44
  1232.0 9.4 collective-permute-start.9
  1335.2 10.2 collective-permute-start.8
  (53 other events, 464.5 us)
Sparse Core Ops, SparseCore 0:
  10.5 56.4 all-gather.19
  69.0 69.8 all-gather.25
  141.1 24.4 all-gather.21
  167.5 69.2 all-gather.23
  238.2 62.6 all-gather.17
  302.3 62.6 all-gather.15
  518.7 65.8 reduce-scatter.16
  643.5 59.3 reduce-scatter.6
  705.3 59.9 reduce-scatter.8
  768.0 66.3 reduce-scatter.14
  838.1 115.0 all-reduce.4
  955.3 23.3 reduce-scatter.12
  982.9 117.7 all-reduce.6
  1103.5 52.6 reduce-scatter.10
  1159.9 72.0 all-reduce.8
  1235.4 99.7 all-reduce.10
